TPU v7x, 512 devices: a whole 4x4x16 slice. The times are simulated.
512 devices in a mesh: dp: 128 (over y, z, core), tensor: 4 (over x).
Axes of the slice: x: 4, y: 4, z: 16, core: 2. Of those that a mesh axis runs over, the one named last changes fastest.
Arguments:
- acts: bfloat16 [8, 32768, 2048], P(None, 'dp', 'tensor'), may hold values from -24 to 24
- out_cot: bfloat16 [8, 32768, 1024], P(None, 'dp', 'tensor'), may hold values from -24 to 24
- emb_ids: int32 [32768], P(('dp', 'tensor')), may hold values from 0 to 8191
- emb_cot: bfloat16 [32768, 1024], P('dp', 'tensor'), may hold values from -24 to 24
- grad_w: float32 [8192, 2048], P(('dp', 'tensor')), may hold values from -6 to 6
- grad_e: float32 [8192, 1024], P(('dp', 'tensor')), may hold values from -6 to 6
Outputs:
- update_w: float32 [8192, 2048], P('dp', 'tensor')
- update_e: float32 [8192, 1024], P(('dp', 'tensor'))
All inputs are finite; a program needn't handle non-finite values. Where the computation divides by a largest or mean magnitude, that divisor is 1e-20 or more.
Results may differ from a plain program's by a relative error of at most 0.0003.
Values sent between devices are 32-bit elements; how exact they have to be, the bound alone decides.
A program may use at most 64 MiB of HBM per device.

v0:
```python
import jax
import jax.numpy as jnp
from jax import lax
from jax.sharding import PartitionSpec as P

HEAD = 64
NS_ITERS = 4
damp_root = 0.7


def newton_inverse(matrices):
    size = matrices.shape[-1]
    eye = jnp.eye(size, dtype=jnp.float32)
    bound = jnp.max(jnp.sum(jnp.abs(matrices), axis=-1), axis=-1)
    approx = eye[None] / bound[:, None, None]
    for sweep in range(NS_ITERS):
        image = jnp.einsum("bij,bjk->bik", matrices, approx, precision=lax.Precision.HIGHEST)
        approx = jnp.einsum(
            "bij,bjk->bik", approx, 2.0 * eye[None] - image, precision=lax.Precision.HIGHEST
        )
    return approx


def local(acts, out_cot, emb_ids, emb_cot, grad_w, grad_e):
    n_dp = lax.axis_size("dp")
    n_tp = lax.axis_size("tensor")
    layers, tok_rows, inner_part = acts.shape
    width_part = out_cot.shape[2]
    heads_part = inner_part // HEAD
    groups_part = width_part // HEAD
    tokens_all = tok_rows * n_dp
    width = width_part * n_tp
    inner = inner_part * n_tp
    groups_all = width // HEAD
    rows_e = grad_e.shape[0]
    vocab = rows_e * n_dp * n_tp
    dp_index = lax.axis_index("dp")
    flat_index = dp_index * n_tp + lax.axis_index("tensor")
    tile_rows = grad_w.shape[0] * n_tp
    block_rows = tile_rows // HEAD
    layer_rows = min(tile_rows, width)
    layer_span = tile_rows // layer_rows
    first_layer = dp_index * tile_rows // width
    split_acts = acts.reshape(layers, tok_rows, heads_part, HEAD)
    gram_a = jnp.einsum(
        "lthi,lthj->lhij", split_acts, split_acts, preferred_element_type=jnp.float32
    )
    split_cot = out_cot.reshape(layers, tok_rows, groups_part, HEAD)
    gram_g = jnp.einsum("lthi,lthj->lhij", split_cot, split_cot, preferred_element_type=jnp.float32)
    split_emb = emb_cot.reshape(tok_rows, groups_part, HEAD)
    gram_e = jnp.einsum("thi,thj->hij", split_emb, split_emb, preferred_element_type=jnp.float32)
    blocks = jnp.concatenate(
        [gram_a.reshape(-1, HEAD, HEAD), gram_g.reshape(-1, HEAD, HEAD), gram_e], axis=0
    )
    block_count = blocks.shape[0]
    diagonal_sums = jnp.trace(blocks, axis1=1, axis2=2)
    local_a = jnp.sum(diagonal_sums[: layers * heads_part].reshape(layers, heads_part), axis=1)
    local_g = jnp.sum(
        diagonal_sums[layers * heads_part : layers * (heads_part + groups_part)].reshape(
            layers, groups_part
        ),
        axis=1,
    )
    local_e = jnp.sum(diagonal_sums[layers * (heads_part + groups_part) :])
    trace_local = jnp.concatenate([local_a, local_g, local_e[None]])
    local_counts = jnp.sum(
        (emb_ids[:, None] == jnp.arange(vocab, dtype=jnp.int32)[None, :]).astype(jnp.float32),
        axis=0,
    )
    traces, counts_all = lax.psum((trace_local, local_counts), ("dp", "tensor"))
    counts_mine = lax.dynamic_slice_in_dim(counts_all, flat_index * rows_e, rows_e)
    trace_a = traces[:layers]
    trace_g = traces[layers : 2 * layers]
    trace_e = traces[2 * layers]
    ratio = jnp.sqrt(trace_a / (tokens_all * inner) / (trace_g / (tokens_all * width)))
    ratio_e = jnp.sqrt(tokens_all / vocab / (trace_e / (tokens_all * width)))
    shift = jnp.concatenate(
        [
            jnp.repeat(damp_root * ratio, heads_part),
            jnp.repeat(damp_root / ratio, groups_part),
            jnp.full((groups_part,), 1.0, jnp.float32) * (damp_root / ratio_e),
        ]
    )
    eye = jnp.eye(HEAD, dtype=jnp.float32)
    owned = -(-block_count // n_dp)
    slots = owned * n_dp
    padded = jnp.pad(blocks.reshape(block_count, HEAD * HEAD), ((0, slots - block_count), (0, 0)))
    mine = lax.psum_scatter(padded, "dp", scatter_dimension=0, tiled=True)
    shift_pad = jnp.pad(shift, (0, slots - block_count), constant_values=1.0)
    shift_mine = lax.dynamic_slice_in_dim(shift_pad, dp_index * owned, owned)
    damped = mine.reshape(owned, HEAD, HEAD) / tokens_all + shift_mine[:, None, None] * eye
    inverse_mine = newton_inverse(damped)
    gathered = lax.all_gather(inverse_mine.reshape(owned, HEAD * HEAD), "dp", axis=0, tiled=True)
    inverses = gathered[:block_count].reshape(block_count, HEAD, HEAD)
    inv_a = inverses[: layers * heads_part].reshape(layers, heads_part, HEAD, HEAD)
    inv_g_part = inverses[layers * heads_part : layers * (heads_part + groups_part)].reshape(
        layers, groups_part, HEAD * HEAD
    )
    inv_e_part = inverses[layers * (heads_part + groups_part) :].reshape(groups_part, HEAD * HEAD)
    base_layer = 0
    sending = jnp.concatenate(
        [inv_g_part.reshape(layers * groups_part, HEAD * HEAD), inv_e_part], axis=0
    )
    shared = lax.all_gather(sending[None], "tensor", axis=0, tiled=True)
    inv_g = shared[:, : layers * groups_part].reshape(n_tp, layers, groups_part, HEAD, HEAD)
    inv_g = jnp.transpose(inv_g, (1, 0, 2, 3, 4)).reshape(layers * groups_all, HEAD, HEAD)
    inv_e = shared[:, layers * groups_part :].reshape(groups_all, HEAD, HEAD)
    tile = lax.all_to_all(grad_w, "tensor", split_axis=1, concat_axis=0, tiled=True)
    g_sel = lax.dynamic_slice_in_dim(
        inv_g, dp_index * block_rows - base_layer * groups_all, block_rows, 0
    )
    left = jnp.einsum(
        "bij,bjc->bic",
        g_sel,
        tile.reshape(block_rows, HEAD, inner_part),
        precision=lax.Precision.HIGHEST,
    )
    a_sel = lax.dynamic_slice_in_dim(inv_a, first_layer, layer_span, 0)
    right = jnp.einsum(
        "lrhi,lhij->lrhj",
        left.reshape(layer_span, layer_rows, heads_part, HEAD),
        a_sel,
        precision=lax.Precision.HIGHEST,
    )
    update_w = right.reshape(tile_rows, inner_part)
    scaled = jnp.einsum(
        "rgi,gij->rgj",
        grad_e.reshape(rows_e, groups_all, HEAD),
        inv_e,
        precision=lax.Precision.HIGHEST,
    )
    update_e = scaled.reshape(rows_e, width) / (counts_mine + damp_root * ratio_e)[:, None]
    return (update_w, update_e)


def solution(mesh):
    in_specs = (
        P(None, "dp", "tensor"),
        P(None, "dp", "tensor"),
        P(("dp", "tensor")),
        P("dp", "tensor"),
        P(("dp", "tensor"), None),
        P(("dp", "tensor"), None),
    )
    out_specs = (P("dp", "tensor"), P(("dp", "tensor"), None))
    return jax.shard_map(local, mesh=mesh, in_specs=in_specs, out_specs=out_specs, check_vma=False)
```

profile of v0, /device:TPU:1, one launch (start us, length us, event | category | flops | bytes accessed | tf_op | source)
XLA Modules:
  0.0 588.8 jit_solution(13494018394217157497)
XLA Ops:
  7.2 3.9 copy.48
  11.1 3.0 fusion.24
  14.2 1.3 copy.49
  15.5 2.0 fusion.25
  17.8 1.6 concatenate.21
  19.4 1.1 concatenate.22
  20.7 2.9 select_maximum_fusion
  23.7 0.8 fusion
  25.0 0.7 slice_reduce_fusion.1
  25.7 0.3 convert_reduce_fusion
  26.0 0.7 pad_maximum_fusion
  26.7 112.1 %all-reduce.3 = (f32[17]{0:T(128)S(1)}, f32[8192]{0:T(1024)S(1)}) all-reduce(f32[17]{0:T(128)S(1)} %pad_maximum_fusion, f32[8192]{0:T(1024)S(1)} %convert_reduce_fusion), channel_id=1, replica_groups=mesh['dp'=128,'tensor'=4] {'dp','tensor'}, use_global_device_ids=true, to_apply=%region_5.6 | all-reduce | flops 8209 | bytes 65672 | tf_op jit(solution)/shard_map/psum | solution.py:70
  138.8 0.6 slice.50
  140.7 0.6 dynamic_slice.12
  141.2 0.7 fusion.12
  142.0 1.3 dynamic-slice
  143.3 237.0 %all-reduce.6.cloned.1.call-done = f32[128,4096]{1,0:T(8,128)} async-done(((f32[128,4096]{1,0:T(8,128)}), f32[128,4096]{1,0:T(8,128)}) %all-reduce.6.cloned.1.call-update) | async-done | bytes 2097168
  380.3 0.5 broadcast.202
  380.8 2.3 add_reduce_fusion
  383.2 0.8 abs_reduce_fusion
  384.0 0.6 reduce_max.9
  385.3 0.8 convolution_subtract_fusion.3
  386.4 0.2 convolution_subtract_fusion.2
  386.5 0.2 fusion.27
  386.7 0.2 convolution_subtract_fusion.1
  386.9 0.2 fusion.28
  387.0 0.2 convolution_subtract_fusion
  387.2 0.2 fusion.29
  387.4 0.7 reshape.283
  388.1 139.9 %all-gather.6.cloned.1.call-done = f32[128,1,4096]{2,1,0:T(1,128)} async-done(((f32[1,1,4096]{2,1,0:T(1,128)}), f32[128,1,4096]{2,1,0:T(1,128)}) %all-gather.6.cloned.1.call-update) | async-done | bytes 2097168 | tf_op jit(solution)/shard_map/all_gather | solution.py:93
  528.0 1.3 slice_bitcast_fusion
  529.3 1.2 copy.52
  530.5 0.7 copy.64
  531.2 4.0 all-to-all-start
  535.3 4.7 all-to-all-done
  540.1 2.7 slice_reduce_fusion
  542.8 2.2 reshape.272
  545.0 24.2 %all-gather.8.cloned.1.call-done = f32[4,36,4096]{2,1,0:T(8,128)} async-done(((f32[1,36,4096]{2,1,0:T(8,128)}), f32[4,36,4096]{2,1,0:T(8,128)}) %all-gather.8.cloned.1.call-update) | async-done | bytes 2359312 | tf_op jit(solution)/shard_map/all_gather | solution.py:104
  569.1 1.1 slice.59
  570.2 0.3 reshape.279
  570.5 0.6 convolution_bitcast_fusion
  571.2 1.6 slice-done
  572.8 3.0 reshape.274
  575.8 2.5 copy.53
  578.3 0.9 fusion.8
  579.2 1.6 fusion.1
  580.8 0.8 copy.58
  581.5 0.7 broadcast_divide_fusion
  (46 shorter events, 2.4 us)
Async XLA Ops:
  7.2 373.2 %all-reduce.6.cloned.1.call-start = ((), (), s32[]{:S(2)}) async-start(), calls=%async_computation.3 | async-start | bytes 4194304
  11.1 3.0 copy-start.1
  15.5 2.0 copy-start.2
  23.6 2.1 copy-start.5
  23.6 504.4 %all-gather.6.cloned.1.call-start = ((), (), s32[]{:S(2)}) async-start(), calls=%async_computation.1 | async-start | bytes 2113536 | tf_op jit(solution)/shard_map/all_gather | solution.py:93
  142.0 388.5 %copy-start.3 = (f32[16,2048]{1,0:T(8,128)S(1)}, f32[16,2048]{1,0:T(8,128)}, u32[]{:S(2)}) copy-start(f32[16,2048]{1,0:T(8,128)} %param.10) | copy-start | bytes 393220
  386.5 148.6 %copy-start.4 = (f32[16,1024]{1,0:T(8,128)S(1)}, f32[16,1024]{1,0:T(8,128)}, u32[]{:S(2)}) copy-start(f32[16,1024]{1,0:T(8,128)} %param.11) | copy-start | bytes 196612
  388.1 181.0 %all-gather.8.cloned.1.call-start = ((), (), s32[]{:S(2)}) async-start(), calls=%async_computation.2 | async-start | bytes 3276800 | tf_op jit(solution)/shard_map/all_gather | solution.py:104
  528.0 12.1 %copy-start = (f32[128,1,4096]{2,1,0:T(1,128)S(1)}, f32[128,1,4096]{2,1,0:T(1,128)}, u32[]{:S(2)}) copy-start(f32[128,1,4096]{2,1,0:T(1,128)} %all-gather.6.cloned.1.call-done) | copy-start | bytes 6291460
  531.2 8.8 %all-to-all-start = ((f32[16,4,512]{2,0,1:T(8,128)}), f32[16,4,512]{2,0,1:T(8,128)S(1)}, u32[]{:S(2)}, u32[]{:S(2)}) async-start(f32[16,4,512]{2,0,1:T(8,128)} %bitcast.65), calls=%async_computation | async-start | bytes 262144 | tf_op jit(solution)/shard_map/all_to_all | solution.py:108
  571.2 1.6 slice-start
Sparse Core Ops, SparseCore 0:
  23.7 356.5 all-reduce.5
  388.2 139.7 all-gather.5
  530.6 38.4 all-gather.7
where the time goes:
time: 589 us
  waiting for transfers between devices  406 us (69%)
  blocking collectives  112 us (19%)
  local copies, waits for them, and re-layouts  30.4 us (5%)
  between operations  15.5 us (3%)
  other arithmetic  11 us (2%)
  matrix products  10.1 us (2%)
    unnamed x4, waiting for transfers between devices  237 us
    all_gather x1, waiting for transfers between devices, local(): lax.all_gather(inverse_mine.reshape(owned, HEAD * HEAD), 'dp', axis=0, ti...  140 us
    psum x1, blocking collectives, local(): traces, counts_all = lax.psum((trace_local, local_counts), ('dp', 'tensor'))  112 us
    all_gather x1, waiting for transfers between devices, local(): shared = lax.all_gather(sending[None], 'tensor', axis=0, tiled=True)  24.2 us
  transfers between devices with their start and end apart: 4, of which 4 were waited for; matrix products, arithmetic and copies ran while one was open for 2% of the time, Pallas kernels for 0%

commit v1 on v0

--- a/solution.py
+++ b/solution.py
@@ -90,7 +90,12 @@
     shift_mine = lax.dynamic_slice_in_dim(shift_pad, dp_index * owned, owned)
     damped = mine.reshape(owned, HEAD, HEAD) / tokens_all + shift_mine[:, None, None] * eye
     inverse_mine = newton_inverse(damped)
-    gathered = lax.all_gather(inverse_mine.reshape(owned, HEAD * HEAD), "dp", axis=0, tiled=True)
+    gathered = jnp.concatenate(
+        lax.all_to_all(
+            jnp.stack([inverse_mine.reshape(owned, HEAD * HEAD)] * lax.axis_size("dp")), "dp", 0, 0
+        ),
+        axis=0,
+    )
     inverses = gathered[:block_count].reshape(block_count, HEAD, HEAD)
     inv_a = inverses[: layers * heads_part].reshape(layers, heads_part, HEAD, HEAD)
     inv_g_part = inverses[layers * heads_part : layers * (heads_part + groups_part)].reshape(

time: 589 us -> 561 us (0.952)
  waiting for transfers between devices: 406 us -> 263 us
  blocking collectives: 112 us -> 225 us
    all_gather x1 -> x0, waiting for transfers between devices: 140 us -> none  [local(): lax.all_gather(inverse_mine.reshape(owned, HEAD * HEAD), 'dp', axis=0, ti...]
    all_to_all x0 -> x1, blocking collectives: none -> 113 us  [local(): lax.all_to_all(jnp.stack([inverse_mine.reshape(owned, HEAD * HEAD)] * lax...]
    unnamed x4 -> x3, waiting for transfers between devices: 237 us -> 237 us
  transfers between devices with their start and end apart: 4 -> 3, of which waited for: 4 -> 3; matrix products, arithmetic and copies ran while one was open for 2% -> 2% of each run, Pallas kernels for 0% -> 0%
where the time goes in v1:
time: 561 us; the launch traced here: 560 us
  waiting for transfers between devices  263 us (47%)
  blocking collectives  225 us (40%)
  local copies, waits for them, and re-layouts  29.7 us (5%)
  between operations  15.8 us (3%)
  other arithmetic  11.9 us (2%)
  matrix products  10.1 us (2%)
    unnamed x3, waiting for transfers between devices  237 us
    all_to_all x1, blocking collectives, local(): lax.all_to_all(jnp.stack([inverse_mine.reshape(owned, HEAD * HEAD)] * lax...  113 us
    psum x1, blocking collectives, local(): traces, counts_all = lax.psum((trace_local, local_counts), ('dp', 'tensor'))  112 us
    all_gather x1, waiting for transfers between devices, local(): shared = lax.all_gather(sending[None], 'tensor', axis=0, tiled=True)  21.7 us
  transfers between devices with their start and end apart: 3, of which 3 were waited for; matrix products, arithmetic and copies ran while one was open for 2% of the time, Pallas kernels for 0%

profile of v1, /device:TPU:1, one launch (start us, length us, event | category | flops | bytes accessed | tf_op | source)
XLA Modules:
  0.0 559.9 jit_solution(15863594401988175615)
XLA Ops:
  7.2 3.9 copy.43
  11.1 3.0 fusion.24
  14.2 1.3 copy.44
  15.5 2.0 fusion.25
  17.8 1.6 concatenate.21
  19.4 1.1 concatenate.22
  20.7 2.9 select_maximum_fusion
  23.7 0.8 fusion
  25.0 0.7 slice_reduce_fusion.1
  25.7 0.3 convert_reduce_fusion
  26.0 0.7 pad_maximum_fusion
  26.7 112.1 %all-reduce.3 = (f32[17]{0:T(128)S(1)}, f32[8192]{0:T(1024)S(1)}) all-reduce(f32[17]{0:T(128)S(1)} %pad_maximum_fusion, f32[8192]{0:T(1024)S(1)} %convert_reduce_fusion), channel_id=1, replica_groups=mesh['dp'=128,'tensor'=4] {'dp','tensor'}, use_global_device_ids=true, to_apply=%region_5.6 | all-reduce | flops 8209 | bytes 65672 | tf_op jit(solution)/shard_map/psum | solution.py:70
  138.8 0.6 slice.54
  140.7 0.6 dynamic_slice.12
  141.2 0.7 fusion.12
  142.0 1.3 dynamic-slice
  143.3 237.1 %all-reduce.6.cloned.1.call-done = f32[128,4096]{1,0:T(8,128)} async-done(((f32[128,4096]{1,0:T(8,128)}), f32[128,4096]{1,0:T(8,128)}) %all-reduce.6.cloned.1.call-update) | async-done | bytes 2097168
  380.4 0.5 broadcast.204
  380.9 2.3 add_reduce_fusion
  383.2 0.8 abs_reduce_fusion
  384.1 0.6 reduce_max.9
  385.4 0.8 convolution_subtract_fusion.3
  386.4 0.2 convolution_subtract_fusion.2
  386.6 0.2 fusion.27
  386.8 0.2 convolution_subtract_fusion.1
  386.9 0.2 fusion.28
  387.1 0.2 convolution_subtract_fusion
  387.3 0.2 fusion.29
  387.5 2.1 stack.3
  389.6 112.9 %all_to_all.21 = f32[128,1,4096]{2,1,0:T(1,128)S(1)} all-to-all(f32[128,1,4096]{2,1,0:T(1,128)S(1)} %stack.3), channel_id=1, replica_groups=mesh['dp'=128,'tensor'=4] {'dp'}, dimensions={0} | all-to-all | bytes 4194304 | tf_op jit(solution)/shard_map/all_to_all | solution.py:94
  502.5 0.3 copy.61
  502.9 0.9 maximum_bitcast_fusion
  503.8 0.7 copy.62
  504.5 4.0 all-to-all-start.1
  508.6 4.7 all-to-all-done.1
  513.4 2.7 slice_reduce_fusion
  516.1 2.2 reshape.277
  518.3 21.7 %all-gather.4.cloned.1.call-done = f32[4,36,4096]{2,1,0:T(8,128)} async-done(((f32[1,36,4096]{2,1,0:T(8,128)}), f32[4,36,4096]{2,1,0:T(8,128)}) %all-gather.4.cloned.1.call-update) | async-done | bytes 2359312 | tf_op jit(solution)/shard_map/all_gather | solution.py:109
  540.0 1.1 slice.64
  541.0 0.3 reshape.285
  541.3 0.6 convolution_bitcast_fusion
  542.1 1.6 slice-done
  543.7 3.0 reshape.280
  546.6 2.5 copy.47
  549.1 0.9 fusion.8
  550.0 1.6 fusion.1
  551.6 0.8 copy.52
  552.3 0.7 broadcast_divide_fusion
  (46 shorter events, 2.5 us)
Async XLA Ops:
  7.2 373.2 %all-reduce.6.cloned.1.call-start = ((), (), s32[]{:S(2)}) async-start(), calls=%async_computation.3 | async-start | bytes 4194304
  11.1 3.0 copy-start
  15.5 2.0 copy-start.1
  23.6 2.1 copy-start.4
  23.6 516.3 %all-gather.4.cloned.1.call-start = ((), (), s32[]{:S(2)}) async-start(), calls=%async_computation.2 | async-start | bytes 3276800 | tf_op jit(solution)/shard_map/all_gather | solution.py:109
  502.5 1.4 copy-start.2
  502.5 6.0 %copy-start.3 = (f32[16,1024]{1,0:T(8,128)S(1)}, f32[16,1024]{1,0:T(8,128)}, u32[]{:S(2)}) copy-start(f32[16,1024]{1,0:T(8,128)} %param.11) | copy-start | bytes 196612
  504.5 8.8 %all-to-all-start.1 = ((f32[16,4,512]{2,0,1:T(8,128)}), f32[16,4,512]{2,0,1:T(8,128)S(1)}, u32[]{:S(2)}, u32[]{:S(2)}) async-start(f32[16,4,512]{2,0,1:T(8,128)} %bitcast.70), calls=%async_computation.1 | async-start | bytes 262144 | tf_op jit(solution)/shard_map/all_to_all | solution.py:113
  542.1 1.6 slice-start
Sparse Core Ops, SparseCore 0:
  23.7 356.6 all-reduce.5
  504.0 35.9 all-gather.3
